TPU v7x, 32 devices: a whole 2x2x4 slice. The times are simulated.
32 devices in a mesh: row: 4 (over y, core), col: 8 (over z, x).
Axes of the slice: x: 2, y: 2, z: 4, core: 2. Of those that a mesh axis runs over, the one named last changes fastest.
Arguments:
- states_now: float32 [40, 4096], P(None, ('col', 'row')), may hold values from -60 to 60
- states_next: float32 [40, 4096], P(None, ('row', 'col')), may hold values from -60 to 60
- states_last: float32 [40, 4096], P(None, ('col', 'row')), may hold values from -60 to 60
- payoff_now: bfloat16 [64, 4096], P(None, ('col', 'row')), may hold values from 0 to 2
- payoff_next: bfloat16 [64, 4096], P(None, ('row', 'col')), may hold values from 0 to 2
- payoff_last: bfloat16 [64, 4096], P(None, ('col', 'row')), may hold values from 0 to 2
Outputs:
- value_next: float32 [64, 4096], P(None, ('row', 'col'))
- value_now: float32 [64, 4096], P(None, ('col', 'row'))
All inputs are finite; a program needn't handle non-finite values.
Results may differ from a plain program's by a relative error of at most 0.0003.
Values sent between devices are 32-bit elements; how exact they have to be, the bound alone decides.
No kernel may reach another device: no remote copies, remote signals or barrier semaphores. Data moves between devices by JAX's collectives and lax.ppermute only.
A program may use at most 128 MiB of HBM per device.

v0:
```python
import math
import jax
import jax.numpy as jnp
from jax import lax
from jax.sharding import PartitionSpec as P


def merged(array, axis, combine):
    everything = jax.tree.map(lambda part: lax.all_gather(part, axis), array)
    first = jax.tree.map(lambda part: part[0], everything)

    def lap(k, so_far):
        return combine(so_far, jax.tree.map(lambda part: part[k], everything))

    return lax.fori_loop(1, lax.axis_size(axis), lap, first)


def log_kernel(row_states, col_states, row_norms, col_norms):
    cross_term = lax.dot_general(
        row_states,
        col_states,
        (((0,), (0,)), ((), ())),
        precision=lax.Precision.HIGHEST,
        preferred_element_type=jnp.float32,
    )
    return cross_term - 0.5 * row_norms[:, None] - 0.5 * col_norms[None, :]


def log_blocks(row_states, col_states):
    factors, points = row_states.shape
    block_rows = math.gcd(points, 512)
    block_count = points // block_rows
    blocks = row_states.reshape(factors, block_count, block_rows).transpose(1, 0, 2)
    norms = jnp.sum(row_states * row_states, axis=0).reshape(block_count, block_rows)
    col_norms = jnp.sum(col_states * col_states, axis=0)

    def build(block_item):
        row_piece, piece_norms = block_item
        return log_kernel(row_piece, col_states, piece_norms, col_norms)

    return lax.map(build, (blocks, norms))


def local_stats(log_weight):
    col_peak = jnp.max(log_weight, axis=(0, 1))
    col_sum = jnp.sum(jnp.exp(log_weight - col_peak[None, None, :]), axis=(0, 1))
    return (col_peak, col_sum)


def join_stats(earlier_pair, later_pair):
    new_peak = jnp.maximum(earlier_pair[0], later_pair[0])
    joined = earlier_pair[1] * jnp.exp(earlier_pair[0] - new_peak) + later_pair[1] * jnp.exp(
        later_pair[0] - new_peak
    )
    return (new_peak, joined)


def stats_row(col_peak, col_sum):
    global_peak = lax.pmax(col_peak, "row")
    global_sum = lax.psum(col_sum * jnp.exp(col_peak - global_peak), "row")
    return (global_peak, global_sum)


def stats_col(col_peak, col_sum):
    return merged((col_peak, col_sum), "col", join_stats)


def continuation(log_weight, later_value, col_peak, col_sum):
    scaled = (later_value / col_sum[None, :]).astype(jnp.bfloat16)

    def project(weight_block):
        kernel = jnp.exp(weight_block - col_peak[None, :]).astype(jnp.bfloat16)
        return lax.dot_general(
            scaled, kernel, (((1,), (1,)), ((), ())), preferred_element_type=jnp.float32
        )

    pieces = lax.map(project, log_weight)
    block_count, block_rows = (log_weight.shape[0], log_weight.shape[1])
    return pieces.transpose(1, 0, 2).reshape(scaled.shape[0], block_count * block_rows)


def per_device(states_now, states_next, states_last, payoff_now, payoff_next, payoff_last):
    own_points = payoff_next.shape[1]
    later_states, later_values = (
        lax.all_gather(states_last, "row", axis=1, tiled=True),
        lax.all_gather(payoff_last.astype(jnp.float32), "row", axis=1, tiled=True),
    )
    next_rows, next_payoff = (
        lax.all_gather(states_next, "col", axis=1, tiled=True),
        lax.all_gather(payoff_next.astype(jnp.float32), "col", axis=1, tiled=True),
    )
    weights = log_blocks(next_rows, later_states)
    col_peak, col_sum = local_stats(weights)
    col_peak, col_sum = stats_row(col_peak, col_sum)
    partial_value = continuation(weights, later_values, col_peak, col_sum)
    whole_sum = lax.psum(partial_value, "col")
    value_block = jnp.maximum(next_payoff, whole_sum)
    value_next = lax.dynamic_slice_in_dim(
        value_block, lax.axis_index("col") * own_points, own_points, 1
    )
    now_rows = lax.all_gather(states_now, "row", axis=1, tiled=True)
    weights = log_blocks(now_rows, next_rows)
    col_peak, col_sum = local_stats(weights)
    col_peak, col_sum = stats_col(col_peak, col_sum)
    partial_value = continuation(weights, value_block, col_peak, col_sum)
    own_block = lax.psum_scatter(partial_value, "row", scatter_dimension=1, tiled=True)
    value_now = jnp.maximum(payoff_now.astype(jnp.float32), own_block)
    return (value_next, value_now)


def solution(mesh):
    in_specs = (
        P(None, ("col", "row")),
        P(None, ("row", "col")),
        P(None, ("col", "row")),
        P(None, ("col", "row")),
        P(None, ("row", "col")),
        P(None, ("col", "row")),
    )
    out_specs = (P(None, ("row", "col")), P(None, ("col", "row")))
    return jax.shard_map(
        per_device, mesh=mesh, in_specs=in_specs, out_specs=out_specs, check_vma=False
    )
```

profile of v0, /device:TPU:0, one launch (start us, length us, event | category | flops | bytes accessed | tf_op | source)
XLA Modules:
  0.0 198.5 jit_solution(9412907396690079252)
XLA Ops:
  7.2 0.0 all-reduce.2.cloned.1.call-start
  7.2 32.6 %all_gather.28 = f32[40,1024]{1,0:T(8,128)S(1)} all-gather(f32[40,128]{1,0:T(8,128)} %param.13), channel_id=1, replica_groups=mesh['row'=4,'col'=8] {'col'}, dimensions={1}, use_global_device_ids=true | all-gather | bytes 184320 | tf_op jit(solution)/shard_map/all_gather | solution.py:89
  39.8 0.1 reshape.54
  40.0 5.5 %all_gather.29 = f32[40,512]{1,0:T(8,128)S(1)} all-gather(f32[40,128]{1,0:T(8,128)} %param.14), channel_id=1, replica_groups=mesh['row'=4,'col'=8] {'row'}, dimensions={1}, use_global_device_ids=true | all-gather | bytes 102400 | tf_op jit(solution)/shard_map/all_gather | solution.py:85
  45.5 2.4 %while.45 = (s32[]{:T(128)}, f32[2,512,512]{2,1,0:T(8,128)S(1)}, f32[2,40,512]{2,0,1:T(2,128)S(1)}, f32[40,512]{1,0:T(8,128)S(1)}, f32[2,512]{1,0:T(2,128)S(1)}, /*index=5*/f32[512]{0:T(512)S(1)}, s32[]{:T(128)}) while((s32[]{:T(128)}, f32[2,512,512]{2,1,0:T(8,128)S(1)}, f32[2,40,512]{2,0,1:T(2,128)S(1)}, f32[40,512]{1,0:T(8,128)S(1)}, ...), condition=%wide.region_3.4_spmd, body=%wide.region_2.3_spmd.sunk | while | flops 126354432 | bytes 1388633 | solution.py:41
  45.5 0.1 constant_dynamic-slice_fusion.6
  45.6 1.1 fusion.23
  46.7 0.1 constant_dynamic-slice_fusion.6
  46.8 1.1 fusion.23
  47.9 0.0 copy-start.1
  47.9 0.2 reduce_max.18
  48.1 0.4 exponential_reduce_fusion.1
  48.5 7.1 %pmax.7 = f32[512]{0:T(512)S(1)} all-reduce(f32[512]{0:T(512)S(1)} %reduce_max.18), channel_id=1, replica_groups=mesh['row'=4,'col'=8] {'row'}, use_global_device_ids=true, to_apply=%region_5.6 | all-reduce | flops 512 | bytes 4096 | tf_op jit(solution)/shard_map/pmax | solution.py:59
  55.6 5.9 %psum.14 = f32[512]{0:T(512)S(1)} all-reduce(f32[512]{0:T(512)S(1)} %exponential_multiply_fusion), channel_id=1, replica_groups=mesh['row'=4,'col'=8] {'row'}, use_global_device_ids=true, to_apply=%region_7.8 | all-reduce | flops 512 | bytes 4096 | tf_op jit(solution)/shard_map/psum | solution.py:60
  61.5 0.0 copy-done.1
  61.5 5.4 %all_gather.30 = f32[64,512]{1,0:T(8,128)S(1)} all-gather(f32[64,128]{1,0:T(8,128)S(1)} %convert_element_type.23), channel_id=1, replica_groups=mesh['row'=4,'col'=8] {'row'}, dimensions={1}, use_global_device_ids=true | all-gather | bytes 163840 | tf_op jit(solution)/shard_map/all_gather | solution.py:86
  66.9 0.0 copy-start
  66.9 0.6 while.46
  66.9 0.3 fusion.26
  67.3 0.3 fusion.26
  67.6 0.7 copy.14
  68.3 0.0 all-reduce.2.cloned.1.call-update
  68.3 0.0 reduce-scatter.2.cloned.1.call-start
  68.4 0.0 copy-done
  68.4 5.3 %all_gather.31 = f32[40,512]{1,0:T(8,128)S(1)} all-gather(f32[40,128]{1,0:T(8,128)S(1)} %copy-done), channel_id=1, replica_groups=mesh['row'=4,'col'=8] {'row'}, dimensions={1}, use_global_device_ids=true | all-gather | bytes 102400 | tf_op jit(solution)/shard_map/all_gather | solution.py:101
  73.7 0.0 copy-start.2
  73.7 2.0 fusion.12
  75.7 0.3 exponential_reduce_fusion
  76.0 30.6 %all-gather.1 = f32[8192]{0:T(1024)S(1)} all-gather(f32[1024]{0:T(1024)S(1)} %exponential_reduce_fusion), channel_id=3, replica_groups=mesh['row'=4,'col'=8] {'col'}, dimensions={0}, use_global_device_ids=true | all-gather | bytes 36864 | tf_op jit(solution)/shard_map/all_gather | solution.py:9
  106.6 30.7 %all-gather = f32[8192]{0:T(1024)S(1)} all-gather(f32[1024]{0:T(1024)S(1)} %get-tuple-element.279), channel_id=2, replica_groups=mesh['row'=4,'col'=8] {'col'}, dimensions={0}, use_global_device_ids=true | all-gather | bytes 36864 | tf_op jit(solution)/shard_map/all_gather | solution.py:9
  137.4 0.0 copy-start.3
  137.4 0.4 while.47
  137.8 0.0 copy-done.2
  137.8 30.7 %all_gather.27 = f32[64,1024]{1,0:T(8,128)S(1)} all-gather(f32[64,128]{1,0:T(8,128)S(1)} %convert_element_type.22), channel_id=1, replica_groups=mesh['row'=4,'col'=8] {'col'}, dimensions={1}, use_global_device_ids=true | all-gather | bytes 294912 | tf_op jit(solution)/shard_map/all_gather | solution.py:90
  168.6 0.0 all-reduce.2.cloned.1.call-done
  168.6 1.0 max.18
  169.6 1.1 fusion.9
  170.6 0.0 reduce-scatter.2.cloned.1.call-update
  170.7 0.6 constant_dynamic-slice_fusion.3
  171.3 19.0 %reduce-scatter.2.cloned.1.call-done = f32[64,128]{1,0:T(8,128)} async-done(((f32[64,512]{1,0:T(8,128)}), f32[64,128]{1,0:T(8,128)}) %reduce-scatter.2.cloned.1.call-update) | async-done | bytes 32784 | tf_op jit(solution)/shard_map/reduce_scatter | solution.py:106
  190.3 0.0 copy-done.3
  190.3 1.4 convert_maximum_fusion
  (34 shorter events, 0.4 us)
Async XLA Ops:
  7.2 161.4 %all-reduce.2.cloned.1.call-start = ((), (), s32[]{:S(2)}) async-start(), calls=%async_computation.1 | async-start | bytes 524288 | tf_op jit(solution)/shard_map/psum | solution.py:96
  47.9 13.6 %copy-start.1 = (bf16[64,128]{1,0:T(8,128)(2,1)S(1)}, bf16[64,128]{1,0:T(8,128)(2,1)}, u32[]{:S(2)}) copy-start(bf16[64,128]{1,0:T(8,128)(2,1)} %param.17) | copy-start | bytes 49156
  66.9 1.5 copy-start
  68.3 122.0 %reduce-scatter.2.cloned.1.call-start = ((), (), s32[]{:S(2)}) async-start(), calls=%async_computation.2 | async-start | bytes 163840 | tf_op jit(solution)/shard_map/reduce_scatter | solution.py:106
  73.7 64.1 %copy-start.2 = (bf16[64,128]{1,0:T(8,128)(2,1)S(1)}, bf16[64,128]{1,0:T(8,128)(2,1)}, u32[]{:S(2)}) copy-start(bf16[64,128]{1,0:T(8,128)(2,1)} %param.16) | copy-start | bytes 49156
  137.4 52.9 %copy-start.3 = (bf16[64,128]{1,0:T(8,128)(2,1)S(1)}, bf16[64,128]{1,0:T(8,128)(2,1)}, u32[]{:S(2)}) copy-start(bf16[64,128]{1,0:T(8,128)(2,1)} %param.15) | copy-start | bytes 49156
Sparse Core Ops, SparseCore 0:
  68.4 71.0 all-reduce.1
  170.8 19.4 reduce-scatter.1
where the time goes:
time: 199 us
  blocking collectives  154 us (77%)
  waiting for transfers between devices  19 us (10%)
  between operations  14.2 us (7%)
  matrix products  5.77 us (3%)
  other arithmetic  3.48 us (2%)
    all_gather x2, blocking collectives, merged(): everything = jax.tree.map(lambda part: lax.all_gather(part, axis), array)  61.3 us
    all_gather x1, blocking collectives, per_device(): lax.all_gather(states_next, 'col', axis=1, tiled=True)  32.6 us
    all_gather x1, blocking collectives, per_device(): lax.all_gather(payoff_next.astype(jnp.float32), 'col', axis=1, tiled=True)  30.7 us
    reduce_scatter x1, waiting for transfers between devices, per_device(): lax.psum_scatter(partial_value, 'row', scatter_dimension=1, tiled=True)  19 us
    pmax x1, blocking collectives, stats_row(): global_peak = lax.pmax(col_peak, 'row')  7.11 us
    psum x1, blocking collectives, stats_row(): global_sum = lax.psum(col_sum * jnp.exp(col_peak - global_peak), 'row')  5.88 us
    all_gather x1, blocking collectives, per_device(): lax.all_gather(states_last, 'row', axis=1, tiled=True)  5.49 us
    all_gather x1, blocking collectives, per_device(): lax.all_gather(payoff_last.astype(jnp.float32), 'row', axis=1, tiled=True)  5.42 us
  transfers between devices with their start and end apart: 2, of which 1 were waited for; matrix products, arithmetic and copies ran while one was open for 2% of the time, Pallas kernels for 0%

commit v1 on v0

--- a/solution.py
+++ b/solution.py
@@ -87,7 +87,12 @@
     )
     next_rows, next_payoff = (
         lax.all_gather(states_next, "col", axis=1, tiled=True),
-        lax.all_gather(payoff_next.astype(jnp.float32), "col", axis=1, tiled=True),
+        jnp.concatenate(
+            lax.all_to_all(
+                jnp.stack([payoff_next.astype(jnp.float32)] * lax.axis_size("col")), "col", 0, 0
+            ),
+            axis=1,
+        ),
     )
     weights = log_blocks(next_rows, later_states)
     col_peak, col_sum = local_stats(weights)

time: 199 us -> 175 us (0.88)
  blocking collectives: 154 us -> 124 us
  starting transfers between devices: 0.08 us -> 5.55 us
    all_gather x1 -> x0, blocking collectives: 30.7 us -> none  [per_device(): lax.all_gather(payoff_next.astype(jnp.float32), 'col', axis=1, tiled=True)]
    all_to_all x0 -> x1, starting transfers between devices: none -> 5.48 us  [per_device(): lax.all_to_all(jnp.stack([payoff_next.astype(jnp.float32)] * lax.axis_siz...]
  transfers between devices with their start and end apart: 2 -> 3, of which waited for: 1 -> 1; matrix products, arithmetic and copies ran while one was open for 2% -> 2% of each run, Pallas kernels for 0% -> 0%
where the time goes in v1:
time: 175 us
  blocking collectives  124 us (71%)
  waiting for transfers between devices  19.2 us (11%)
  between operations  14.2 us (8%)
  matrix products  5.76 us (3%)
  starting transfers between devices  5.55 us (3%)
  other arithmetic  3.49 us (2%)
  local copies, waits for them, and re-layouts  2.5 us (1%)
    all_gather x2, blocking collectives, merged(): everything = jax.tree.map(lambda part: lax.all_gather(part, axis), array)  61.8 us
    all_gather x1, blocking collectives, per_device(): lax.all_gather(states_next, 'col', axis=1, tiled=True)  32.6 us
    reduce_scatter x1, waiting for transfers between devices, per_device(): lax.psum_scatter(partial_value, 'row', scatter_dimension=1, tiled=True)  19.1 us
    pmax x1, blocking collectives, stats_row(): global_peak = lax.pmax(col_peak, 'row')  7.11 us
    psum x1, blocking collectives, stats_row(): global_sum = lax.psum(col_sum * jnp.exp(col_peak - global_peak), 'row')  5.88 us
    all_gather x1, blocking collectives, per_device(): lax.all_gather(states_last, 'row', axis=1, tiled=True)  5.49 us
    all_to_all x1, starting transfers between devices, per_device(): lax.all_to_all(jnp.stack([payoff_next.astype(jnp.float32)] * lax.axis_siz...  5.48 us
    all_gather x1, blocking collectives, per_device(): lax.all_gather(payoff_last.astype(jnp.float32), 'row', axis=1, tiled=True)  5.42 us
  transfers between devices with their start and end apart: 3, of which 1 were waited for; matrix products, arithmetic and copies ran while one was open for 2% of the time, Pallas kernels for 0%

profile of v1, /device:TPU:0, one launch (start us, length us, event | category | flops | bytes accessed | tf_op | source)
XLA Modules:
  0.0 174.5 jit_solution(16604641671554591684)
XLA Ops:
  7.2 0.0 all-reduce.2.cloned.1.call-start
  7.2 32.6 %all_gather.24 = f32[40,1024]{1,0:T(8,128)S(1)} all-gather(f32[40,128]{1,0:T(8,128)} %param.13), channel_id=1, replica_groups=mesh['row'=4,'col'=8] {'col'}, dimensions={1}, use_global_device_ids=true | all-gather | bytes 184320 | tf_op jit(solution)/shard_map/all_gather | solution.py:89
  39.8 0.1 reshape.64
  40.0 5.5 %all_gather.25 = f32[40,512]{1,0:T(8,128)S(1)} all-gather(f32[40,128]{1,0:T(8,128)} %param.14), channel_id=1, replica_groups=mesh['row'=4,'col'=8] {'row'}, dimensions={1}, use_global_device_ids=true | all-gather | bytes 102400 | tf_op jit(solution)/shard_map/all_gather | solution.py:85
  45.5 2.4 %while.45 = (s32[]{:T(128)}, f32[2,512,512]{2,1,0:T(8,128)S(1)}, f32[2,40,512]{2,0,1:T(2,128)S(1)}, f32[40,512]{1,0:T(8,128)S(1)}, f32[2,512]{1,0:T(2,128)S(1)}, /*index=5*/f32[512]{0:T(512)S(1)}, s32[]{:T(128)}) while((s32[]{:T(128)}, f32[2,512,512]{2,1,0:T(8,128)S(1)}, f32[2,40,512]{2,0,1:T(2,128)S(1)}, f32[40,512]{1,0:T(8,128)S(1)}, ...), condition=%wide.region_3.4_spmd, body=%wide.region_2.3_spmd.sunk | while | flops 126354432 | bytes 1388633 | solution.py:41
  45.5 0.1 constant_dynamic-slice_fusion.6
  45.6 1.1 fusion.24
  46.7 0.1 constant_dynamic-slice_fusion.6
  46.8 1.1 fusion.24
  47.9 0.0 copy-start.1
  47.9 0.2 reduce_max.18
  48.1 0.4 exponential_reduce_fusion.1
  48.5 7.1 %pmax.7 = f32[512]{0:T(512)S(1)} all-reduce(f32[512]{0:T(512)S(1)} %reduce_max.18), channel_id=1, replica_groups=mesh['row'=4,'col'=8] {'row'}, use_global_device_ids=true, to_apply=%region_5.6 | all-reduce | flops 512 | bytes 4096 | tf_op jit(solution)/shard_map/pmax | solution.py:59
  55.6 5.9 %psum.14 = f32[512]{0:T(512)S(1)} all-reduce(f32[512]{0:T(512)S(1)} %exponential_multiply_fusion), channel_id=1, replica_groups=mesh['row'=4,'col'=8] {'row'}, use_global_device_ids=true, to_apply=%region_7.8 | all-reduce | flops 512 | bytes 4096 | tf_op jit(solution)/shard_map/psum | solution.py:60
  61.5 0.0 copy-done.1
  61.5 5.4 %all_gather.26 = f32[64,512]{1,0:T(8,128)S(1)} all-gather(f32[64,128]{1,0:T(8,128)S(1)} %convert_element_type.23), channel_id=1, replica_groups=mesh['row'=4,'col'=8] {'row'}, dimensions={1}, use_global_device_ids=true | all-gather | bytes 163840 | tf_op jit(solution)/shard_map/all_gather | solution.py:86
  66.9 0.0 copy-start.2
  66.9 0.0 copy-start
  66.9 0.6 while.46
  66.9 0.3 fusion.27
  67.3 0.3 fusion.27
  67.6 0.7 copy.18
  68.3 0.0 all-reduce.2.cloned.1.call-update
  68.3 0.0 copy-done.2
  68.3 0.7 stack.2
  69.0 5.5 %all-to-all-start = ((f32[8,64,128]{2,1,0:T(8,128)}), f32[8,64,128]{2,1,0:T(8,128)S(1)}, u32[]{:S(2)}, u32[]{:S(2)}) async-start(f32[8,64,128]{2,1,0:T(8,128)} %stack.2), calls=%async_computation | async-start | bytes 524288 | tf_op jit(solution)/shard_map/all_to_all | solution.py:91
  74.5 0.0 reduce-scatter.2.cloned.1.call-start
  74.6 0.0 copy-done
  74.6 5.3 %all_gather.27 = f32[40,512]{1,0:T(8,128)S(1)} all-gather(f32[40,128]{1,0:T(8,128)S(1)} %copy-done), channel_id=1, replica_groups=mesh['row'=4,'col'=8] {'row'}, dimensions={1}, use_global_device_ids=true | all-gather | bytes 102400 | tf_op jit(solution)/shard_map/all_gather | solution.py:106
  79.9 2.0 %fusion.12 = (f32[1024]{0:T(1024)S(1)}, f32[512,1024]{1,0:T(8,128)S(1)}) fusion(f32[1024]{0:T(1024)S(1)} %broadcast_multiply_fusion.1, f32[512]{0:T(512)S(1)} %broadcast_multiply_fusion.2, f32[40,512]{1,0:T(8,128)S(1)} %all_gather.27, f32[40,1024]{1,0:T(8,128)S(1)} %all_gather.24), kind=kOutput, calls=%fused_computation.36 | convolution fusion | flops 253230080 | bytes 2353152 | tf_op jit(solution)/shard_map/while/body/eval_jaxpr/dot_general | solution.py:19
  81.9 0.3 exponential_reduce_fusion
  82.2 0.0 copy-start.3
  82.2 31.1 %all-gather.1 = f32[8192]{0:T(1024)S(1)} all-gather(f32[1024]{0:T(1024)S(1)} %exponential_reduce_fusion), channel_id=3, replica_groups=mesh['row'=4,'col'=8] {'col'}, dimensions={0}, use_global_device_ids=true | all-gather | bytes 36864 | tf_op jit(solution)/shard_map/all_gather | solution.py:9
  113.4 30.6 %all-gather = f32[8192]{0:T(1024)S(1)} all-gather(f32[1024]{0:T(1024)S(1)} %get-tuple-element.285), channel_id=2, replica_groups=mesh['row'=4,'col'=8] {'col'}, dimensions={0}, use_global_device_ids=true | all-gather | bytes 36864 | tf_op jit(solution)/shard_map/all_gather | solution.py:9
  144.0 0.4 while.47
  144.4 0.0 all-reduce.2.cloned.1.call-done
  144.5 0.0 all-to-all-done
  144.5 1.0 bitcast_maximum_fusion
  145.5 1.1 fusion.9
  146.6 0.0 reduce-scatter.2.cloned.1.call-update
  146.6 0.6 constant_dynamic-slice_fusion.3
  147.2 19.1 %reduce-scatter.2.cloned.1.call-done = f32[64,128]{1,0:T(8,128)} async-done(((f32[64,512]{1,0:T(8,128)}), f32[64,128]{1,0:T(8,128)}) %reduce-scatter.2.cloned.1.call-update) | async-done | bytes 32784 | tf_op jit(solution)/shard_map/reduce_scatter | solution.py:111
  166.3 0.0 copy-done.3
  166.3 1.4 convert_maximum_fusion
  (33 shorter events, 0.4 us)
Async XLA Ops:
  7.2 137.3 %all-reduce.2.cloned.1.call-start = ((), (), s32[]{:S(2)}) async-start(), calls=%async_computation.2 | async-start | bytes 524288 | tf_op jit(solution)/shard_map/psum | solution.py:101
  47.9 13.6 %copy-start.1 = (bf16[64,128]{1,0:T(8,128)(2,1)S(1)}, bf16[64,128]{1,0:T(8,128)(2,1)}, u32[]{:S(2)}) copy-start(bf16[64,128]{1,0:T(8,128)(2,1)} %param.17) | copy-start | bytes 49156
  66.9 1.4 copy-start.2
  66.9 7.7 %copy-start = (f32[40,128]{1,0:T(8,128)S(1)}, f32[40,128]{1,0:T(8,128)}, u32[]{:S(2)}) copy-start(f32[40,128]{1,0:T(8,128)} %param.12) | copy-start | bytes 61444
  69.0 75.4 %all-to-all-start = ((f32[8,64,128]{2,1,0:T(8,128)}), f32[8,64,128]{2,1,0:T(8,128)S(1)}, u32[]{:S(2)}, u32[]{:S(2)}) async-start(f32[8,64,128]{2,1,0:T(8,128)} %stack.2), calls=%async_computation | async-start | bytes 524288 | tf_op jit(solution)/shard_map/all_to_all | solution.py:91
  74.5 91.8 %reduce-scatter.2.cloned.1.call-start = ((), (), s32[]{:S(2)}) async-start(), calls=%async_computation.3 | async-start | bytes 163840 | tf_op jit(solution)/shard_map/reduce_scatter | solution.py:111
  82.2 84.1 %copy-start.3 = (bf16[64,128]{1,0:T(8,128)(2,1)S(1)}, bf16[64,128]{1,0:T(8,128)(2,1)}, u32[]{:S(2)}) copy-start(bf16[64,128]{1,0:T(8,128)(2,1)} %param.15) | copy-start | bytes 49156
Sparse Core Ops, SparseCore 0:
  68.4 72.5 all-reduce.1
  146.7 19.5 reduce-scatter.1
